TPU v7x, 128 devices: a whole 4x4x4 slice. The times are simulated.
128 devices in a mesh: patch: 16 (over y, x), col: 8 (over z, core).
Axes of the slice: x: 4, y: 4, z: 4, core: 2. Of those that a mesh axis runs over, the one named last changes fastest.
Arguments:
- potential0: float32 [512, 16, 128], P(('patch', 'col')), may hold values from -3 to 3
- source_term: float32 [512, 16, 128], P(('patch', 'col')), may hold values from -9 to 9
- self_coef: float32 [512, 128], P(('patch', 'col')), may hold values from 1 to 4
- nearfield: float32 [512, 24, 128, 128], P(('patch', 'col')), may hold values from -0.109375 to 0.109375
- precond: float32 [512, 128, 128], P(('patch', 'col')), may hold values from -1 to 2
- exch_current: float32 [512, 128], P(('patch', 'col')), may hold values from 0.05 to 0.5
- conductance: float32 [512, 128], P(('patch', 'col')), may hold values from 0.1 to 1
- member: int32 [512, 128], P(('patch', 'col')), may hold values from 0 to 63
- anode_drive: float32 [64], replicated, may hold values from -1 to 1
- pair_source: int32 [512, 24], P(('patch', 'col')), may hold values from 0 to 39
- pair_count: int32 [512], P(('patch', 'col')), may hold values from 1 to 24, as said below
Outputs:
- potential: float32 [512, 16, 128], P(('patch', 'col'))
- residual: float32 [512, 16, 128], P(('patch', 'col'))
Inputs may be any that keep to these rules, and one draw needn't show every extreme that they name: Slots k < pair_count[b] of block b are live; some block has all 24 slots live, and the blocks of some devices hold far more live pairs than those of others.
All inputs are finite; a program needn't handle non-finite values.
Results may differ from a plain program's by a relative error of at most 0.0003.
Values sent between devices are 32-bit elements; how exact they have to be, the bound alone decides.
A program may use at most 64 MiB of HBM per device.

v0:
```python
import jax
import jax.numpy as jnp
from jax import lax
from jax.sharding import PartitionSpec as P

NEWTON = 2
GMRES = 2


ALPHA = 0.6
BETA = 0.4
EPS = 1e-06


def from_behind(array, axis, by):
    size = lax.axis_size(axis)
    return lax.ppermute(array, axis, [(i, (i + by) % size) for i in range(size)])


def column_sum(left, right):
    return jnp.sum(left * right, axis=(0, 2))


def least_squares(columns, beta):
    depth = len(columns)
    hessen = jnp.zeros((beta.shape[0], depth + 1, depth), jnp.float32)
    for place in range(depth):
        hessen = hessen.at[:, : place + 2, place].set(columns[place].T)
    gram = jnp.einsum("cij,cik->cjk", hessen, hessen, precision=lax.Precision.HIGHEST)
    right = beta[:, None] * hessen[:, 0, :]
    lower = jnp.linalg.cholesky(gram)
    middle = jax.scipy.linalg.solve_triangular(lower, right[:, :, None], lower=True)
    return jax.scipy.linalg.solve_triangular(lower, middle, lower=True, trans=1)[:, :, 0]


def body(
    potential0,
    source_term,
    self_coef,
    nearfield,
    precond,
    exch_current,
    conductance,
    member,
    anode_drive,
    pair_source,
    pair_count,
):
    pair_slots = pair_source.shape[1]
    live_mask = (jnp.arange(pair_slots, dtype=jnp.int32)[None, :] < pair_count[:, None]).astype(
        jnp.float32
    )
    members = anode_drive.shape[0]
    onehot = (jnp.arange(members, dtype=jnp.int32)[:, None, None] == member[None]).astype(
        jnp.float32
    )
    member_drive = jnp.sum(onehot * anode_drive[:, None, None], axis=0)
    diagonal = self_coef[:, None, :]
    current = exch_current[:, None, :]
    conduct = conductance[:, None, :]

    def near_field(field):
        own_patch = lax.all_gather(field, "col", axis=0, tiled=True)
        before = from_behind(field, "patch", 1)
        following = from_behind(field, "patch", -1)
        stacked = jnp.concatenate([own_patch, before, following], axis=0)
        sources = stacked[pair_source]
        return jnp.einsum(
            "bkij,bkcj->bci",
            nearfield,
            sources * live_mask[:, :, None, None],
            precision=lax.Precision.HIGHEST,
        )

    def mismatch(field, near_value):
        grow = jnp.exp(ALPHA * field)
        shrink = jnp.exp(-BETA * field)
        value = (
            diagonal * field
            + near_value
            + current * (grow - shrink)
            + conduct * (field - member_drive[:, None, :])
            - source_term
        )
        slope = current * (ALPHA * grow + BETA * shrink) + conduct
        return (value, slope)

    field = potential0
    near_now = near_field(field)
    for newton in range(NEWTON):
        value, slope = mismatch(field, near_now)
        start = -value
        beta = jnp.sqrt(lax.psum(column_sum(start, start), ("patch", "col")) + EPS)
        basis = [start / beta[None, :, None]]
        directions = []
        near_images = []
        columns = []
        for step in range(GMRES):
            direction = jnp.einsum(
                "bij,bcj->bci", precond, basis[step], precision=lax.Precision.HIGHEST
            )
            directions.append(direction)
            near_image = near_field(direction)
            near_images.append(near_image)
            image = diagonal * direction + near_image + slope * direction
            coeffs = []
            for place in range(step + 1):
                coeff = lax.psum(column_sum(basis[place], image), ("patch", "col"))
                image = image - coeff[None, :, None] * basis[place]
                coeffs.append(coeff)
            norm = jnp.sqrt(lax.psum(column_sum(image, image), ("patch", "col")) + EPS)
            basis.append(image / norm[None, :, None])
            columns.append(jnp.stack(coeffs + [norm]))
        weights = least_squares(columns, beta)
        update = jnp.zeros_like(field)
        for step in range(GMRES):
            update = update + weights[:, step][None, :, None] * directions[step]
        field = field + update
        near_now = near_field(field)
    final_value, final_slope = mismatch(field, near_now)
    return (field, final_value)


def solution(mesh):
    return jax.shard_map(
        body,
        mesh=mesh,
        in_specs=(
            P(("patch", "col"), None, None),
            P(("patch", "col"), None, None),
            P(("patch", "col"), None),
            P(("patch", "col"), None, None, None),
            P(("patch", "col"), None, None),
            P(("patch", "col"), None),
            P(("patch", "col"), None),
            P(("patch", "col"), None),
            P(),
            P(("patch", "col"), None),
            P(("patch", "col")),
        ),
        out_specs=(P(("patch", "col"), None, None), P(("patch", "col"), None, None)),
        check_vma=False,
    )
```

profile of v0, /device:TPU:1, one launch (start us, length us, event | category | flops | bytes accessed | tf_op | source)
XLA Modules:
  0.0 974.0 jit_solution(4111155873102971596)
XLA Ops:
  0.7 2.1 collective-permute-start
  2.8 3.8 collective-permute-start.1
  6.6 15.1 %all_gather.21 = f32[32,16,128]{2,1,0:T(8,128)S(1)} all-gather(f32[4,16,128]{2,1,0:T(8,128)} %param.24), channel_id=1, replica_groups=mesh['patch'=16,'col'=8] {'col'}, dimensions={0}, use_global_device_ids=true | all-gather | bytes 294912 | tf_op jit(solution)/shard_map/all_gather | solution.py:63
  21.7 0.7 compare_select_fusion
  22.5 0.7 fusion.40
  23.2 0.8 select_reduce_fusion
  24.0 0.7 gather_fusion
  24.7 7.6 multiply_reduce_fusion.11
  32.3 64.2 %psum.84 = f32[16]{0:T(128)S(1)} all-reduce(f32[16]{0:T(128)S(1)} %get-tuple-element.61), channel_id=1, replica_groups=mesh['patch'=16,'col'=8] {'patch','col'}, use_global_device_ids=true, to_apply=%region_2.0 | all-reduce | flops 16 | bytes 128 | tf_op jit(solution)/shard_map/psum | solution.py:93
  96.6 0.6 fusion.43
  97.1 0.2 collective-permute-start.2
  97.3 4.6 collective-permute-start.3
  101.9 13.9 %all_gather.22 = f32[32,16,128]{2,1,0:T(8,128)S(1)} all-gather(f32[4,16,128]{2,1,0:T(8,128)S(1)} %fusion.43), channel_id=1, replica_groups=mesh['patch'=16,'col'=8] {'col'}, dimensions={0}, use_global_device_ids=true | all-gather | bytes 294912 | tf_op jit(solution)/shard_map/all_gather | solution.py:63
  115.8 0.7 gather_fusion.1
  116.5 7.5 multiply_reduce_fusion.10
  124.0 63.4 %psum.85 = f32[16]{0:T(128)S(1)} all-reduce(f32[16]{0:T(128)S(1)} %get-tuple-element.63), channel_id=1, replica_groups=mesh['patch'=16,'col'=8] {'patch','col'}, use_global_device_ids=true, to_apply=%region_4.0 | all-reduce | flops 16 | bytes 128 | tf_op jit(solution)/shard_map/psum | solution.py:108
  187.6 63.0 %psum.86 = f32[16]{0:T(128)S(1)} all-reduce(f32[16]{0:T(128)S(1)} %multiply_reduce_fusion.9), channel_id=1, replica_groups=mesh['patch'=16,'col'=8] {'patch','col'}, use_global_device_ids=true, to_apply=%region_6.0 | all-reduce | flops 16 | bytes 128 | tf_op jit(solution)/shard_map/psum | solution.py:111
  250.6 0.6 fusion.44
  251.2 0.8 collective-permute-start.4
  252.1 4.0 collective-permute-start.5
  256.0 13.8 %all_gather.23 = f32[32,16,128]{2,1,0:T(8,128)S(1)} all-gather(f32[4,16,128]{2,1,0:T(8,128)S(1)} %fusion.44), channel_id=1, replica_groups=mesh['patch'=16,'col'=8] {'col'}, dimensions={0}, use_global_device_ids=true | all-gather | bytes 294912 | tf_op jit(solution)/shard_map/all_gather | solution.py:63
  269.8 0.7 gather_fusion.2
  270.5 7.5 multiply_reduce_fusion.8
  278.0 64.4 %psum.87 = f32[16]{0:T(128)S(1)} all-reduce(f32[16]{0:T(128)S(1)} %get-tuple-element.65), channel_id=1, replica_groups=mesh['patch'=16,'col'=8] {'patch','col'}, use_global_device_ids=true, to_apply=%region_8.0 | all-reduce | flops 16 | bytes 128 | tf_op jit(solution)/shard_map/psum | solution.py:108
  342.4 0.2 multiply_reduce_fusion.7
  342.6 62.5 %psum.88 = f32[16]{0:T(128)S(1)} all-reduce(f32[16]{0:T(128)S(1)} %multiply_reduce_fusion.7), channel_id=1, replica_groups=mesh['patch'=16,'col'=8] {'patch','col'}, use_global_device_ids=true, to_apply=%region_10.0 | all-reduce | flops 16 | bytes 128 | tf_op jit(solution)/shard_map/psum | solution.py:108
  405.1 0.2 multiply_reduce_fusion.6
  405.3 64.0 %psum.89 = f32[16]{0:T(128)S(1)} all-reduce(f32[16]{0:T(128)S(1)} %multiply_reduce_fusion.6), channel_id=1, replica_groups=mesh['patch'=16,'col'=8] {'patch','col'}, use_global_device_ids=true, to_apply=%region_12.0 | all-reduce | flops 16 | bytes 128 | tf_op jit(solution)/shard_map/psum | solution.py:111
  469.5 0.2 fusion.47
  469.7 0.2 copy.89
  470.0 3.1 custom-call.12
  473.3 3.0 custom-call.14
  476.7 4.8 collective-permute-start.7
  481.5 14.5 %all_gather.24 = f32[32,16,128]{2,1,0:T(8,128)S(1)} all-gather(f32[4,16,128]{2,1,0:T(8,128)S(1)} %add_add_fusion.1), channel_id=1, replica_groups=mesh['patch'=16,'col'=8] {'col'}, dimensions={0}, use_global_device_ids=true | all-gather | bytes 294912 | tf_op jit(solution)/shard_map/all_gather | solution.py:63
  496.0 0.7 gather_fusion.3
  496.7 7.5 multiply_reduce_fusion.5
  504.2 61.8 %psum.90 = f32[16]{0:T(128)S(1)} all-reduce(f32[16]{0:T(128)S(1)} %get-tuple-element.67), channel_id=1, replica_groups=mesh['patch'=16,'col'=8] {'patch','col'}, use_global_device_ids=true, to_apply=%region_16.0 | all-reduce | flops 16 | bytes 128 | tf_op jit(solution)/shard_map/psum | solution.py:93
  566.0 0.6 fusion.45
  566.6 1.2 collective-permute-start.8
  567.7 3.7 collective-permute-start.9
  571.4 13.9 %all_gather.25 = f32[32,16,128]{2,1,0:T(8,128)S(1)} all-gather(f32[4,16,128]{2,1,0:T(8,128)S(1)} %fusion.45), channel_id=1, replica_groups=mesh['patch'=16,'col'=8] {'col'}, dimensions={0}, use_global_device_ids=true | all-gather | bytes 294912 | tf_op jit(solution)/shard_map/all_gather | solution.py:63
  585.3 0.7 gather_fusion.4
  586.0 7.5 multiply_reduce_fusion.4
  593.5 63.5 %psum.91 = f32[16]{0:T(128)S(1)} all-reduce(f32[16]{0:T(128)S(1)} %get-tuple-element.69), channel_id=1, replica_groups=mesh['patch'=16,'col'=8] {'patch','col'}, use_global_device_ids=true, to_apply=%region_18.0 | all-reduce | flops 16 | bytes 128 | tf_op jit(solution)/shard_map/psum | solution.py:108
  657.1 62.6 %psum.92 = f32[16]{0:T(128)S(1)} all-reduce(f32[16]{0:T(128)S(1)} %multiply_reduce_fusion.3), channel_id=1, replica_groups=mesh['patch'=16,'col'=8] {'patch','col'}, use_global_device_ids=true, to_apply=%region_20.0 | all-reduce | flops 16 | bytes 128 | tf_op jit(solution)/shard_map/psum | solution.py:111
  719.7 0.6 fusion.46
  720.2 0.8 collective-permute-start.10
  721.1 4.0 collective-permute-start.11
  725.0 14.0 %all_gather.26 = f32[32,16,128]{2,1,0:T(8,128)S(1)} all-gather(f32[4,16,128]{2,1,0:T(8,128)S(1)} %fusion.46), channel_id=1, replica_groups=mesh['patch'=16,'col'=8] {'col'}, dimensions={0}, use_global_device_ids=true | all-gather | bytes 294912 | tf_op jit(solution)/shard_map/all_gather | solution.py:63
  739.1 0.7 gather_fusion.5
  739.8 7.5 multiply_reduce_fusion.2
  747.2 64.4 %psum.93 = f32[16]{0:T(128)S(1)} all-reduce(f32[16]{0:T(128)S(1)} %get-tuple-element.71), channel_id=1, replica_groups=mesh['patch'=16,'col'=8] {'patch','col'}, use_global_device_ids=true, to_apply=%region_22.0 | all-reduce | flops 16 | bytes 128 | tf_op jit(solution)/shard_map/psum | solution.py:108
  811.6 0.2 multiply_reduce_fusion.1
  811.8 62.5 %psum.94 = f32[16]{0:T(128)S(1)} all-reduce(f32[16]{0:T(128)S(1)} %multiply_reduce_fusion.1), channel_id=1, replica_groups=mesh['patch'=16,'col'=8] {'patch','col'}, use_global_device_ids=true, to_apply=%region_24.0 | all-reduce | flops 16 | bytes 128 | tf_op jit(solution)/shard_map/psum | solution.py:108
  874.3 0.2 multiply_reduce_fusion
  874.5 64.0 %psum.95 = f32[16]{0:T(128)S(1)} all-reduce(f32[16]{0:T(128)S(1)} %multiply_reduce_fusion), channel_id=1, replica_groups=mesh['patch'=16,'col'=8] {'patch','col'}, use_global_device_ids=true, to_apply=%region_26.0 | all-reduce | flops 16 | bytes 128 | tf_op jit(solution)/shard_map/psum | solution.py:111
  938.7 0.2 fusion.48
  939.0 0.2 copy.100
  939.2 3.1 custom-call.15
  942.6 3.0 custom-call.17
  946.0 4.8 collective-permute-start.13
  950.8 14.3 %all_gather.27 = f32[32,16,128]{2,1,0:T(8,128)S(1)} all-gather(f32[4,16,128]{2,1,0:T(8,128)S(1)} %add_add_fusion), channel_id=1, replica_groups=mesh['patch'=16,'col'=8] {'col'}, dimensions={0}, use_global_device_ids=true | all-gather | bytes 294912 | tf_op jit(solution)/shard_map/all_gather | solution.py:63
  965.1 0.7 gather_fusion.6
  965.8 8.0 fusion.3
  (83 shorter events, 2.3 us)
Async XLA Ops:
  0.6 95.9 %copy-start = (f32[4,128,128]{2,1,0:T(8,128)S(1)}, f32[4,128,128]{2,1,0:T(8,128)}, u32[]{:S(2)}) copy-start(f32[4,128,128]{2,1,0:T(8,128)} %param.28) | copy-start | bytes 786436
  0.6 115.9 %copy-start.1 = (f32[4,16,128]{2,1,0:T(8,128)S(1)}, f32[4,16,128]{2,1,0:T(8,128)}, u32[]{:S(2)}) copy-start(f32[4,16,128]{2,1,0:T(8,128)} %param.24) | copy-start | bytes 98308
  0.7 115.9 %copy-start.6 = (f32[4,128]{1,0:T(4,128)S(1)}, f32[4,128]{1,0:T(4,128)}, u32[]{:S(2)}) copy-start(f32[4,128]{1,0:T(4,128)} %param.26) | copy-start | bytes 6148
  0.7 115.9 %copy-start.5 = (f32[4,128]{1,0:T(4,128)S(1)}, f32[4,128]{1,0:T(4,128)}, u32[]{:S(2)}) copy-start(f32[4,128]{1,0:T(4,128)} %param.29) | copy-start | bytes 6148
  0.7 115.9 %copy-start.4 = (f32[4,128]{1,0:T(4,128)S(1)}, f32[4,128]{1,0:T(4,128)}, u32[]{:S(2)}) copy-start(f32[4,128]{1,0:T(4,128)} %param.30) | copy-start | bytes 6148
  0.7 23.3 %collective-permute-start = (f32[4,16,128]{2,1,0:T(8,128)}, f32[4,16,128]{2,1,0:T(8,128)S(1)}, u32[]{:S(2)}, u32[]{:S(2)}) collective-permute-start(f32[4,16,128]{2,1,0:T(8,128)} %param.24), channel_id=1, source_target_pairs={{0,8},{8,16},{16,24},{24,32},{32,40},{40,48},{48,56},{56,64},{64,7... | collective-permute-start | bytes 98312 | tf_op jit(solution)/shard_map/ppermute | solution.py:17
  2.8 21.2 %collective-permute-start.1 = (f32[4,16,128]{2,1,0:T(8,128)}, f32[4,16,128]{2,1,0:T(8,128)S(1)}, u32[]{:S(2)}, u32[]{:S(2)}) collective-permute-start(f32[4,16,128]{2,1,0:T(8,128)} %param.24), channel_id=1, source_target_pairs={{0,120},{8,0},{16,8},{24,16},{32,24},{40,32},{48,40},{56,48},{64,5... | collective-permute-start | bytes 98312 | tf_op jit(solution)/shard_map/ppermute | solution.py:17
  97.1 18.7 %collective-permute-start.2 = (f32[4,16,128]{2,1,0:T(8,128)S(1)}, f32[4,16,128]{2,1,0:T(8,128)S(1)}, u32[]{:S(2)}, u32[]{:S(2)}) collective-permute-start(f32[4,16,128]{2,1,0:T(8,128)S(1)} %fusion.43), channel_id=1, source_target_pairs={{0,8},{8,16},{16,24},{24,32},{32,40},{40,48},{48,56},{56,64},{64,7... | collective-permute-start | bytes 98312 | tf_op jit(solution)/shard_map/ppermute | solution.py:17
  97.3 18.4 %collective-permute-start.3 = (f32[4,16,128]{2,1,0:T(8,128)S(1)}, f32[4,16,128]{2,1,0:T(8,128)S(1)}, u32[]{:S(2)}, u32[]{:S(2)}) collective-permute-start(f32[4,16,128]{2,1,0:T(8,128)S(1)} %fusion.43), channel_id=1, source_target_pairs={{0,120},{8,0},{16,8},{24,16},{32,24},{40,32},{48,40},{56,48},{64,5... | collective-permute-start | bytes 98312 | tf_op jit(solution)/shard_map/ppermute | solution.py:17
  251.2 18.6 %collective-permute-start.4 = (f32[4,16,128]{2,1,0:T(8,128)S(1)}, f32[4,16,128]{2,1,0:T(8,128)S(1)}, u32[]{:S(2)}, u32[]{:S(2)}) collective-permute-start(f32[4,16,128]{2,1,0:T(8,128)S(1)} %fusion.44), channel_id=1, source_target_pairs={{0,8},{8,16},{16,24},{24,32},{32,40},{40,48},{48,56},{56,64},{64,7... | collective-permute-start | bytes 98312 | tf_op jit(solution)/shard_map/ppermute | solution.py:17
  252.1 17.7 %collective-permute-start.5 = (f32[4,16,128]{2,1,0:T(8,128)S(1)}, f32[4,16,128]{2,1,0:T(8,128)S(1)}, u32[]{:S(2)}, u32[]{:S(2)}) collective-permute-start(f32[4,16,128]{2,1,0:T(8,128)S(1)} %fusion.44), channel_id=1, source_target_pairs={{0,120},{8,0},{16,8},{24,16},{32,24},{40,32},{48,40},{56,48},{64,5... | collective-permute-start | bytes 98312 | tf_op jit(solution)/shard_map/ppermute | solution.py:17
  269.8 226.9 %copy-start.2 = (f32[4,16,128]{2,1,0:T(8,128)S(1)}, f32[4,16,128]{2,1,0:T(8,128)}, u32[]{:S(2)}) copy-start(f32[4,16,128]{2,1,0:T(8,128)} %param.25) | copy-start | bytes 98308
  476.7 19.3 %collective-permute-start.6 = (f32[4,16,128]{2,1,0:T(8,128)S(1)}, f32[4,16,128]{2,1,0:T(8,128)S(1)}, u32[]{:S(2)}, u32[]{:S(2)}) collective-permute-start(f32[4,16,128]{2,1,0:T(8,128)S(1)} %add_add_fusion.1), channel_id=1, source_target_pairs={{0,8},{8,16},{16,24},{24,32},{32,40},{40,48},{48,56},{56,64},{64,7... | collective-permute-start | bytes 98312 | tf_op jit(solution)/shard_map/ppermute | solution.py:17
  476.7 19.3 %collective-permute-start.7 = (f32[4,16,128]{2,1,0:T(8,128)S(1)}, f32[4,16,128]{2,1,0:T(8,128)S(1)}, u32[]{:S(2)}, u32[]{:S(2)}) collective-permute-start(f32[4,16,128]{2,1,0:T(8,128)S(1)} %add_add_fusion.1), channel_id=1, source_target_pairs={{0,120},{8,0},{16,8},{24,16},{32,24},{40,32},{48,40},{56,48},{64,5... | collective-permute-start | bytes 98312 | tf_op jit(solution)/shard_map/ppermute | solution.py:17
  566.6 18.7 %collective-permute-start.8 = (f32[4,16,128]{2,1,0:T(8,128)S(1)}, f32[4,16,128]{2,1,0:T(8,128)S(1)}, u32[]{:S(2)}, u32[]{:S(2)}) collective-permute-start(f32[4,16,128]{2,1,0:T(8,128)S(1)} %fusion.45), channel_id=1, source_target_pairs={{0,8},{8,16},{16,24},{24,32},{32,40},{40,48},{48,56},{56,64},{64,7... | collective-permute-start | bytes 98312 | tf_op jit(solution)/shard_map/ppermute | solution.py:17
  567.7 17.5 %collective-permute-start.9 = (f32[4,16,128]{2,1,0:T(8,128)S(1)}, f32[4,16,128]{2,1,0:T(8,128)S(1)}, u32[]{:S(2)}, u32[]{:S(2)}) collective-permute-start(f32[4,16,128]{2,1,0:T(8,128)S(1)} %fusion.45), channel_id=1, source_target_pairs={{0,120},{8,0},{16,8},{24,16},{32,24},{40,32},{48,40},{56,48},{64,5... | collective-permute-start | bytes 98312 | tf_op jit(solution)/shard_map/ppermute | solution.py:17
  720.2 18.8 %collective-permute-start.10 = (f32[4,16,128]{2,1,0:T(8,128)S(1)}, f32[4,16,128]{2,1,0:T(8,128)S(1)}, u32[]{:S(2)}, u32[]{:S(2)}) collective-permute-start(f32[4,16,128]{2,1,0:T(8,128)S(1)} %fusion.46), channel_id=1, source_target_pairs={{0,8},{8,16},{16,24},{24,32},{32,40},{40,48},{48,56},{56,64},{64,7... | collective-permute-start | bytes 98312 | tf_op jit(solution)/shard_map/ppermute | solution.py:17
  721.1 17.9 %collective-permute-start.11 = (f32[4,16,128]{2,1,0:T(8,128)S(1)}, f32[4,16,128]{2,1,0:T(8,128)S(1)}, u32[]{:S(2)}, u32[]{:S(2)}) collective-permute-start(f32[4,16,128]{2,1,0:T(8,128)S(1)} %fusion.46), channel_id=1, source_target_pairs={{0,120},{8,0},{16,8},{24,16},{32,24},{40,32},{48,40},{56,48},{64,5... | collective-permute-start | bytes 98312 | tf_op jit(solution)/shard_map/ppermute | solution.py:17
  945.9 27.9 %copy-start.3 = (f32[4,16,128]{2,1,0:T(8,128)}, f32[4,16,128]{2,1,0:T(8,128)S(1)}, u32[]{:S(2)}) copy-start(f32[4,16,128]{2,1,0:T(8,128)S(1)} %add_add_fusion) | copy-start | bytes 98308
  945.9 19.2 %collective-permute-start.12 = (f32[4,16,128]{2,1,0:T(8,128)S(1)}, f32[4,16,128]{2,1,0:T(8,128)S(1)}, u32[]{:S(2)}, u32[]{:S(2)}) collective-permute-start(f32[4,16,128]{2,1,0:T(8,128)S(1)} %add_add_fusion), channel_id=1, source_target_pairs={{0,8},{8,16},{16,24},{24,32},{32,40},{40,48},{48,56},{56,64},{64,7... | collective-permute-start | bytes 98312 | tf_op jit(solution)/shard_map/ppermute | solution.py:17
  946.0 19.1 %collective-permute-start.13 = (f32[4,16,128]{2,1,0:T(8,128)S(1)}, f32[4,16,128]{2,1,0:T(8,128)S(1)}, u32[]{:S(2)}, u32[]{:S(2)}) collective-permute-start(f32[4,16,128]{2,1,0:T(8,128)S(1)} %add_add_fusion), channel_id=1, source_target_pairs={{0,120},{8,0},{16,8},{24,16},{32,24},{40,32},{48,40},{56,48},{64,5... | collective-permute-start | bytes 98312 | tf_op jit(solution)/shard_map/ppermute | solution.py:17
where the time goes:
time: 984 us; the launch traced here: 974 us
  blocking collectives  860 us (87%)
  matrix products  55.7 us (6%)
  starting transfers between devices  34.8 us (4%)
  other arithmetic  16.5 us (2%)
    psum x6, blocking collectives, body(): coeff = lax.psum(column_sum(basis[place], image), ('patch', 'col'))  381 us
    psum x4, blocking collectives, body(): norm = jnp.sqrt(lax.psum(column_sum(image, image), ('patch', 'col')) + EPS)  254 us
    psum x2, blocking collectives, body(): beta = jnp.sqrt(lax.psum(column_sum(start, start), ('patch', 'col')) + EPS)  126 us
    all_gather x7, blocking collectives, near_field(): own_patch = lax.all_gather(field, 'col', axis=0, tiled=True)  99.4 us
    dot_general x7, matrix products, near_field(): jnp.einsum('bkij,bkcj->bci', nearfield, sources * live_mask[:, :, None, N...  52.9 us
    ppermute x14, starting transfers between devices, from_behind(): lax.ppermute(array, axis, [(i, (i + by) % size) for i in range(size)])  34.8 us
  transfers between devices with their start and end apart: 14, of which 0 were waited for; matrix products, arithmetic and copies ran while one was open for 0% of the time, Pallas kernels for 0%

commit v1 on v0

v1 whole, which is shorter than its diff:
```python
import functools

import jax
import jax.numpy as jnp
from jax import lax
from jax.experimental import pallas as pl
from jax.experimental.pallas import tpu as pltpu
from jax.sharding import PartitionSpec as P

NEWTON = 2

ALPHA = 0.6
BETA = 0.4
EPS = 1e-06

MESH = pl.DeviceIdType.MESH
F32 = jnp.float32
BF16 = jnp.bfloat16


def halves(array):
    high = array.astype(BF16)
    low = (array - high.astype(F32)).astype(BF16)
    return high, low


def both_halves(left, right):
    rows = left.shape[0] // 2
    wide = lax.dot_general(left, right, (((1,), (1,)), ((), ())), preferred_element_type=F32)
    half = wide.shape[1] // 2
    return wide[:rows, :half] + (wide[rows:, :half] + wide[:rows, half:]) + wide[rows:, half:]


def kernel(
    patches,
    cols,
    drive_s,
    source_s,
    count_s,
    potential0_h,
    source_term_h,
    self_coef_h,
    nearfield_h,
    precond_h,
    current_h,
    conduct_h,
    member_h,
    potential_o,
    residual_o,
    potential0,
    source_term,
    panels,
    member,
    staged,
    weights,
    precond_f,
    precond_w,
    exchange,
    split,
    near_out,
    sums_a,
    sums_b,
    load_sem,
    send_sem,
    recv_sem,
    sum_send,
    sum_recv,
):
    patch = lax.axis_index("patch")
    col = lax.axis_index("col")
    blocks, pairs = source_s.shape
    columns = potential0.shape[1]
    slots = exchange.shape[1]

    loads = [
        pltpu.make_async_copy(potential0_h, potential0, load_sem.at[0]),
        pltpu.make_async_copy(source_term_h, source_term, load_sem.at[1]),
        pltpu.make_async_copy(self_coef_h, panels.at[0], load_sem.at[2]),
        pltpu.make_async_copy(current_h, panels.at[1], load_sem.at[3]),
        pltpu.make_async_copy(conduct_h, panels.at[2], load_sem.at[4]),
        pltpu.make_async_copy(member_h, member, load_sem.at[5]),
        pltpu.make_async_copy(precond_h, precond_f, load_sem.at[6]),
    ]
    matrix_loads = [
        pltpu.make_async_copy(nearfield_h.at[b], staged.at[b], load_sem.at[7 + b])
        for b in range(blocks)
    ]
    for load in loads + matrix_loads:
        load.start()

    def peer_col(step):
        return lax.rem(col + step, cols)

    def peer_patch(step):
        return lax.rem(patch + step, patches)

    barrier = pltpu.get_barrier_semaphore()
    for step in range(1, cols):
        pl.semaphore_signal(
            barrier, inc=1, device_id={"col": peer_col(step)}, device_id_type=MESH
        )
    for step in range(1, patches):
        pl.semaphore_signal(
            barrier, inc=1, device_id={"patch": peer_patch(step)}, device_id_type=MESH
        )
    pl.semaphore_wait(barrier, cols + patches - 2)

    own = pl.ds(pl.multiple_of(col * blocks, blocks), blocks)
    before = pl.ds(cols * blocks, blocks)
    after = pl.ds((cols + 1) * blocks, blocks)
    incoming = pl.ds(0, slots - blocks)

    def start_exchange(turn, value):
        exchange[turn, own] = value
        mine = exchange.at[turn, own]

        def send(place, target):
            pltpu.make_async_remote_copy(
                src_ref=mine,
                dst_ref=exchange.at[turn, place],
                send_sem=send_sem.at[turn],
                recv_sem=recv_sem.at[turn],
                device_id=target,
                device_id_type=MESH,
            ).start()

        for step in range(1, cols):
            send(own, {"col": peer_col(step)})
        send(before, {"patch": peer_patch(1)})
        send(after, {"patch": peer_patch(patches - 1)})

    def exchange_copy(turn):
        return pltpu.make_async_remote_copy(
            src_ref=exchange.at[turn, incoming],
            dst_ref=exchange.at[turn, incoming],
            send_sem=send_sem.at[turn],
            recv_sem=recv_sem.at[turn],
            device_id={"col": peer_col(1)},
            device_id_type=MESH,
        )

    def near_field(turn):
        exchange_copy(turn).wait_recv()
        high, low = halves(exchange[turn])
        split[:, :columns] = high
        split[:, columns:] = low

        def block(b, carry):
            left = jnp.concatenate([split[source_s[b, k]] for k in range(pairs)], axis=1)
            near_out[b] = both_halves(left, weights[b])
            return carry

        lax.fori_loop(0, blocks, block, 0)
        return near_out[...]

    def start_sums_a(turn, parts):
        lane = lax.broadcasted_iota(jnp.int32, (columns, 128), 1)
        packed = jnp.zeros((columns, 128), F32)
        for place, (left, right) in enumerate(parts):
            value = jnp.sum(jnp.sum(left * right, axis=0), axis=1, keepdims=True)
            packed = jnp.where(lane == place, value, packed)
        sums_a[turn, patch] = packed
        for step in range(1, patches):
            pltpu.make_async_remote_copy(
                src_ref=sums_a.at[turn, patch],
                dst_ref=sums_a.at[turn, patch],
                send_sem=sum_send.at[0, turn],
                recv_sem=sum_recv.at[0, turn],
                device_id={"patch": peer_patch(step)},
                device_id_type=MESH,
            ).start()

    def sums_copy(stage, turn):
        buffer, size = ((sums_a, patches), (sums_b, cols))[stage]
        return pltpu.make_async_remote_copy(
            src_ref=buffer.at[turn, pl.ds(0, size - 1)],
            dst_ref=buffer.at[turn, pl.ds(0, size - 1)],
            send_sem=sum_send.at[stage, turn],
            recv_sem=sum_recv.at[stage, turn],
            device_id={"col": peer_col(1)},
            device_id_type=MESH,
        )

    def start_sums_b(turn):
        sums_copy(0, turn).wait_recv()
        sums_b[turn, col] = jnp.sum(sums_a[turn], axis=0)
        for step in range(1, cols):
            pltpu.make_async_remote_copy(
                src_ref=sums_b.at[turn, col],
                dst_ref=sums_b.at[turn, col],
                send_sem=sum_send.at[1, turn],
                recv_sem=sum_recv.at[1, turn],
                device_id={"col": peer_col(step)},
                device_id_type=MESH,
            ).start()

    def finish_sums(turn, count):
        sums_copy(1, turn).wait_recv()
        total = jnp.sum(sums_b[turn], axis=0)
        return [
            jnp.broadcast_to(total[:, place : place + 1], (columns, 128))
            for place in range(count)
        ]

    for load in loads:
        load.wait()
    start_exchange(0, potential0[...])

    owner = member[...]
    drive = jnp.zeros(owner.shape, F32)
    for place in range(drive_s.shape[0]):
        drive = jnp.where(owner == place, drive_s[place], drive)
    panels[3] = drive
    high, low = halves(precond_f[...])
    precond_w[:, :128] = high
    precond_w[:, 128:] = low

    for b in range(blocks):
        matrix_loads[b].wait()

        def prepare(k, carry, b=b):
            live = jnp.where(k < count_s[b], 1.0, 0.0).astype(F32)
            high, low = halves(staged[b, k] * live)
            place = pl.ds(pl.multiple_of(k * 128, 128), 128)
            weights[b, :128, place] = high
            weights[b, 128:, place] = low
            return carry

        lax.fori_loop(0, pairs, prepare, 0, unroll=4)

    def panel(place):
        return panels[place][:, None, :]

    def mismatch(field, near_value):
        grow = jnp.exp(ALPHA * field)
        shrink = jnp.exp(-BETA * field)
        value = (
            panel(0) * field
            + near_value
            + panel(1) * (grow - shrink)
            + panel(2) * (field - panel(3))
            - source_term[...]
        )
        slope = panel(1) * (ALPHA * grow + BETA * shrink) + panel(2)
        return value, slope

    def apply_precond(value):
        high, low = halves(value)
        left = jnp.concatenate([high, low], axis=1)
        return jnp.stack([both_halves(left[b], precond_w[b]) for b in range(blocks)])

    field = potential0[...]
    near_now = near_field(0)
    for newton in range(NEWTON):
        turn = 1 + 2 * newton
        value, slope = mismatch(field, near_now)
        p0 = -value
        z0 = apply_precond(p0)
        start_exchange(turn, z0)
        diagonal = panel(0) + slope
        n0 = near_field(turn)
        p1 = diagonal * z0 + n0
        z1 = apply_precond(p1)
        start_exchange(turn + 1, z1)
        start_sums_a(2 * newton, [(p0, p0), (p0, p1)])
        start_sums_b(2 * newton)
        n1 = near_field(turn + 1)
        p2 = diagonal * z1 + n1
        g00, g01 = finish_sums(2 * newton, 2)
        beta2 = g00 + EPS
        h00 = g01 / beta2
        c = p1 - h00[None] * p0
        q = p2 - h00[None] * p1
        start_sums_a(2 * newton + 1, [(c, c), (p0, q), (c, q), (q, q)])
        start_sums_b(2 * newton + 1)
        cc, pq, cq, qq = finish_sums(2 * newton + 1, 4)
        beta = jnp.sqrt(beta2)
        pc = g01 - h00 * g00
        h10 = jnp.sqrt(cc / beta2 + EPS)
        scale = 1.0 / (beta * h10)
        scale2 = scale * scale
        v00 = g00 / beta2
        v01 = pc / beta * scale
        v11 = cc * scale2
        w0 = pq / beta * scale
        w1 = cq * scale2
        ww = qq * scale2
        h01 = w0
        h11 = w1 - h01 * v01
        square = (
            ww
            + h01 * h01 * v00
            + h11 * h11 * v11
            - 2.0 * h01 * w0
            - 2.0 * h11 * w1
            + 2.0 * h01 * h11 * v01
        )
        square = jnp.maximum(square, 0.0) + EPS
        gram0 = h00 * h00 + h10 * h10
        gram1 = h00 * h01 + h10 * h11
        gram2 = h01 * h01 + h11 * h11 + square
        lower0 = jnp.sqrt(gram0)
        lower1 = gram1 / lower0
        lower2 = jnp.sqrt(gram2 - lower1 * lower1)
        middle0 = beta * h00 / lower0
        middle1 = (beta * h01 - lower1 * middle0) / lower2
        y1 = middle1 / lower2
        y0 = (middle0 - lower1 * y1) / lower0
        a1 = y1 * scale
        a0 = y0 / beta - a1 * h00
        field = field + (a0[None] * z0 + a1[None] * z1)
        near_now = near_now + (a0[None] * n0 + a1[None] * n1)
    potential_o[...] = field
    residual_o[...] = mismatch(field, near_now)[0]

    for turn in range(2 * NEWTON + 1):
        exchange_copy(turn).wait_send()
    for turn in range(2 * NEWTON):
        sums_copy(0, turn).wait_send()
        sums_copy(1, turn).wait_send()


def body(patches, cols, potential0, source_term, self_coef, nearfield, precond, exch_current, conductance, member, anode_drive, pair_source, pair_count):
    blocks, columns, panels = potential0.shape
    pairs = nearfield.shape[1]
    turns = 2 * NEWTON + 1
    slots = (cols + 2) * blocks
    smem = pl.BlockSpec(memory_space=pltpu.SMEM)
    hbm = pl.BlockSpec(memory_space=pl.ANY)
    vmem = pl.BlockSpec(memory_space=pltpu.VMEM)
    out = jax.ShapeDtypeStruct((blocks, columns, panels), F32)
    return pl.pallas_call(
        functools.partial(kernel, patches, cols),
        out_shape=(out, out),
        in_specs=[smem] * 3 + [hbm] * 8,
        out_specs=(vmem, vmem),
        scratch_shapes=[
            pltpu.VMEM((blocks, columns, panels), F32),
            pltpu.VMEM((blocks, columns, panels), F32),
            pltpu.VMEM((4, blocks, panels), F32),
            pltpu.VMEM((blocks, panels), jnp.int32),
            pltpu.VMEM((blocks, pairs, panels, panels), F32),
            pltpu.VMEM((blocks, 2 * panels, pairs * panels), BF16),
            pltpu.VMEM((blocks, panels, panels), F32),
            pltpu.VMEM((blocks, 2 * panels, panels), BF16),
            pltpu.VMEM((turns, slots, columns, panels), F32),
            pltpu.VMEM((slots, 2 * columns, panels), BF16),
            pltpu.VMEM((blocks, columns, panels), F32),
            pltpu.VMEM((2 * NEWTON, patches, columns, 128), F32),
            pltpu.VMEM((2 * NEWTON, cols, columns, 128), F32),
            pltpu.SemaphoreType.DMA((7 + blocks,)),
            pltpu.SemaphoreType.DMA((turns,)),
            pltpu.SemaphoreType.DMA((turns,)),
            pltpu.SemaphoreType.DMA((2, 2 * NEWTON)),
            pltpu.SemaphoreType.DMA((2, 2 * NEWTON)),
        ],
        compiler_params=pltpu.CompilerParams(
            collective_id=0, has_side_effects=True, vmem_limit_bytes=40 * 1024 * 1024
        ),
        name="newton_gmres",
    )(
        anode_drive,
        pair_source,
        pair_count,
        potential0,
        source_term,
        self_coef,
        nearfield,
        precond,
        exch_current,
        conductance,
        member,
    )


def solution(mesh):
    both = ("patch", "col")
    return jax.shard_map(
        functools.partial(body, mesh.shape["patch"], mesh.shape["col"]),
        mesh=mesh,
        in_specs=(
            P(both, None, None),
            P(both, None, None),
            P(both, None),
            P(both, None, None, None),
            P(both, None, None),
            P(both, None),
            P(both, None),
            P(both, None),
            P(),
            P(both, None),
            P(both),
        ),
        out_specs=(P(both, None, None), P(both, None, None)),
        check_vma=False,
    )
```

time: 984 us -> 82.5 us (0.08)
  blocking collectives: 860 us -> 0 us
  Pallas kernels: 0 us -> 70.2 us
  matrix products: 55.7 us -> 0 us
  starting transfers between devices: 34.8 us -> 0 us
  other arithmetic: 16.5 us -> 0 us
    psum x12 -> x0, blocking collectives: 760 us -> none  [the longest x6 381 us: body(): coeff = lax.psum(column_sum(basis[place], image), ('patch', 'col'))]
    all_gather x7 -> x0, blocking collectives: 99.4 us -> none  [near_field(): own_patch = lax.all_gather(field, 'col', axis=0, tiled=True)]
    pallas_call x0 -> x1, Pallas kernels: none -> 70.2 us  [body(): pl.pallas_call(functools.partial(kernel, patches, cols), out_shape=(out,...]
    dot_general x13 -> x0, matrix products: 55.7 us -> none  [the longest x7 52.9 us: near_field(): jnp.einsum('bkij,bkcj->bci', nearfield, sources * live_mask[:, :, None, N...]
    ppermute x14 -> x0, starting transfers between devices: 34.8 us -> none  [from_behind(): lax.ppermute(array, axis, [(i, (i + by) % size) for i in range(size)])]
    another operation x24 -> x0, other arithmetic: 12.7 us -> none  [the longest x7 6.39 us: least_squares(): lower = jnp.linalg.cholesky(gram)]
    unnamed x16 -> x24, local copies, waits for them, and re-layouts: 0.22 us -> 11.2 us
  transfers between devices with their start and end apart: 14 -> 0, of which waited for: 0 -> 0; matrix products, arithmetic and copies ran while one was open for 0% -> 0% of each run, Pallas kernels for 0% -> 0%
where the time goes in v1:
time: 82.5 us; the launch traced here: 82 us
  Pallas kernels  70.2 us (85%)
  local copies, waits for them, and re-layouts  11.2 us (14%)
    pallas_call x1, Pallas kernels, body(): pl.pallas_call(functools.partial(kernel, patches, cols), out_shape=(out,...  70.2 us
    unnamed x24, local copies, waits for them, and re-layouts  11.2 us

profile of v1, /device:TPU:1, one launch (start us, length us, event | category | flops | bytes accessed | tf_op | source)
XLA Modules:
  0.0 82.0 jit_solution(14698721973704172631)
XLA Ops:
  0.6 0.0 copy-start
  0.6 2.8 %copy-done = f32[4,24,128,128]{3,2,1,0:T(8,128)S(1)} copy-done((f32[4,24,128,128]{3,2,1,0:T(8,128)S(1)}, f32[4,24,128,128]{3,2,1,0:T(8,128)}, u32[]{:S(2)}) %copy-start) | copy-done | bytes 6291480
  3.4 0.0 copy-start.1
  3.4 0.9 %copy-done.1 = f32[4,128,128]{2,1,0:T(8,128)S(1)} copy-done((f32[4,128,128]{2,1,0:T(8,128)S(1)}, f32[4,128,128]{2,1,0:T(8,128)}, u32[]{:S(2)}) %copy-start.1) | copy-done | bytes 262168
  4.4 0.0 copy-start.2
  4.4 0.8 copy-done.2
  5.1 0.0 copy-start.3
  5.1 0.8 copy-done.3
  5.9 0.0 copy-start.4
  5.9 0.7 copy-done.4
  6.6 0.0 copy-start.5
  6.6 0.7 copy-done.5
  7.3 0.0 copy-start.6
  7.3 0.7 copy-done.6
  7.9 0.0 copy-start.7
  7.9 0.7 copy-done.7
  8.6 0.0 copy-start.8
  8.6 0.7 copy-done.8
  9.3 0.0 copy-start.9
  9.3 0.7 copy-done.9
  10.0 0.0 copy-start.10
  10.0 0.7 copy-done.10
  10.6 70.2 %newton_gmres.1 = (f32[4,16,128]{2,1,0:T(8,128)S(1)}, f32[4,16,128]{2,1,0:T(8,128)S(1)}) custom-call(f32[64]{0:T(128)S(1)} %copy-done.9, s32[4,24]{1,0:T(4,128)S(1)} %copy-done.4, s32[4]{0:T(128)S(1)} %copy-done.10, f32[4,16,128]{2,1,0:T(8,128)S(1)} %copy-done.2, f32[4,16,128]{2,1,0:T(8,128)S(1)} %copy-done.3, f32[4,128]{1,0:T(4,128)S(1)} %copy-done.5, ...), custom_call_target="tpu_custom_call" | custom-call | tf_op jit(solution)/shard_map/newton_gmres/pallas_call | solution.py:332
  80.8 0.6 copy.15
  81.4 0.6 copy.16
Async XLA Ops:
  0.6 2.8 %copy-start = (f32[4,24,128,128]{3,2,1,0:T(8,128)S(1)}, f32[4,24,128,128]{3,2,1,0:T(8,128)}, u32[]{:S(2)}) copy-start(f32[4,24,128,128]{3,2,1,0:T(8,128)} %nearfield_h.1) | copy-start | bytes 18874372
  3.4 0.9 %copy-start.1 = (f32[4,128,128]{2,1,0:T(8,128)S(1)}, f32[4,128,128]{2,1,0:T(8,128)}, u32[]{:S(2)}) copy-start(f32[4,128,128]{2,1,0:T(8,128)} %precond_h.1) | copy-start | bytes 786436
  4.4 0.8 copy-start.2
  5.1 0.8 copy-start.3
  5.9 0.7 copy-start.4
  6.6 0.7 copy-start.5
  7.3 0.7 copy-start.6
  7.9 0.7 copy-start.7
  8.6 0.7 copy-start.8
  9.3 0.7 copy-start.9
  10.0 0.7 copy-start.10

commit v2 on v1

v2 whole, which is shorter than its diff:
```python
import functools

import jax
import jax.numpy as jnp
from jax import lax
from jax.experimental import pallas as pl
from jax.experimental.pallas import tpu as pltpu
from jax.sharding import PartitionSpec as P

NEWTON = 2

ALPHA = 0.6
BETA = 0.4
EPS = 1e-06

MESH = pl.DeviceIdType.MESH
F32 = jnp.float32
BF16 = jnp.bfloat16


def halves(array):
    high = array.astype(BF16)
    low = (array - high.astype(F32)).astype(BF16)
    return high, low


def both_halves(left, right):
    rows = left.shape[0] // 2
    wide = jnp.dot(left, right, preferred_element_type=F32)
    half = wide.shape[1] // 2
    return wide[:rows, :half] + (wide[rows:, :half] + wide[:rows, half:]) + wide[rows:, half:]


def kernel(
    patches,
    cols,
    drive_h,
    source_h,
    count_h,
    potential0_h,
    source_term_h,
    self_coef_h,
    nearfield_h,
    precond_h,
    current_h,
    conduct_h,
    member_h,
    potential_o,
    residual_o,
    drive_s,
    source_s,
    count_s,
    potential0,
    source_term,
    panels,
    member,
    staged,
    weights,
    precond_f,
    precond_w,
    exchange,
    split,
    sums,
    load_sem,
    send_sem,
    recv_sem,
    sum_send,
    sum_recv,
):
    patch = lax.axis_index("patch")
    col = lax.axis_index("col")
    blocks, pairs = source_s.shape
    columns = potential0.shape[1]
    slots = exchange.shape[1]

    loads = [
        pltpu.make_async_copy(potential0_h, potential0, load_sem.at[0]),
        pltpu.make_async_copy(source_term_h, source_term, load_sem.at[1]),
        pltpu.make_async_copy(self_coef_h, panels.at[0], load_sem.at[2]),
        pltpu.make_async_copy(current_h, panels.at[1], load_sem.at[3]),
        pltpu.make_async_copy(conduct_h, panels.at[2], load_sem.at[4]),
        pltpu.make_async_copy(member_h, member, load_sem.at[5]),
        pltpu.make_async_copy(precond_h, precond_f, load_sem.at[6]),
        pltpu.make_async_copy(drive_h, drive_s, load_sem.at[7]),
        pltpu.make_async_copy(source_h, source_s, load_sem.at[8]),
        pltpu.make_async_copy(count_h, count_s, load_sem.at[9]),
    ]
    matrix_loads = [
        pltpu.make_async_copy(nearfield_h.at[b], staged.at[b], load_sem.at[10 + b])
        for b in range(blocks)
    ]
    for load in loads + matrix_loads:
        load.start()

    me = patch * cols + col
    devices = patches * cols

    def peer_col(step):
        return lax.rem(col + step, cols)

    def peer_patch(step):
        return lax.rem(patch + step, patches)

    def everyone():
        def distance(step, size):
            return min(step, size - step)

        steps = [(p, c) for p in range(patches) for c in range(cols) if p or c]
        side = 4
        steps.sort(
            key=lambda s: (
                distance(s[0] // side, patches // side)
                + distance(s[0] % side, side)
                + distance(s[1] // 2, cols // 2)
            ),
            reverse=True,
        )
        near_patch = [peer_patch(p) for p in range(patches)]
        near_col = [peer_col(c) for c in range(cols)]
        return [(near_patch[p], near_col[c]) for p, c in steps]

    others = everyone()
    barrier = pltpu.get_barrier_semaphore()
    for target in others:
        pl.semaphore_signal(barrier, inc=1, device_id=target, device_id_type=MESH)
    pl.semaphore_wait(barrier, devices - 1)

    own = pl.ds(pl.multiple_of(col * blocks, blocks), blocks)
    before = pl.ds(cols * blocks, blocks)
    after = pl.ds((cols + 1) * blocks, blocks)
    incoming = pl.ds(0, slots - blocks)

    def start_exchange(turn, value):
        exchange[turn, own] = value
        mine = exchange.at[turn, own]

        def send(place, target):
            pltpu.make_async_remote_copy(
                src_ref=mine,
                dst_ref=exchange.at[turn, place],
                send_sem=send_sem.at[turn],
                recv_sem=recv_sem.at[turn],
                device_id=target,
                device_id_type=MESH,
            ).start()

        steps = sorted(range(1, cols), key=lambda s: -min(s // 2, cols // 2 - s // 2))
        for step in steps:
            send(own, {"col": peer_col(step)})
        send(before, {"patch": peer_patch(1)})
        send(after, {"patch": peer_patch(patches - 1)})

    def exchange_copy(turn):
        return pltpu.make_async_remote_copy(
            src_ref=exchange.at[turn, incoming],
            dst_ref=exchange.at[turn, incoming],
            send_sem=send_sem.at[turn],
            recv_sem=recv_sem.at[turn],
            device_id={"col": peer_col(1)},
            device_id_type=MESH,
        )

    def near_field(turn):
        exchange_copy(turn).wait_recv()
        high, low = halves(exchange[turn])
        split[:, :columns] = high
        split[:, columns:] = low

        results = []
        for b in range(blocks):
            left = jnp.concatenate([split[source_s[b, k]] for k in range(pairs)], axis=1)
            results.append(both_halves(left, weights[b]))
        return jnp.stack(results)

    def start_sums(turn, parts):
        rows = [jnp.sum(left * right, axis=0) for left, right in parts]
        rows.append(jnp.zeros((128 - len(parts) * columns, 128), F32))
        table = jnp.concatenate(rows, axis=0)
        sums[turn, me] = jnp.sum(table.T, axis=0, keepdims=True)
        for target in others:
            pltpu.make_async_remote_copy(
                src_ref=sums.at[turn, me],
                dst_ref=sums.at[turn, me],
                send_sem=sum_send.at[turn],
                recv_sem=sum_recv.at[turn],
                device_id=target,
                device_id_type=MESH,
            ).start()

    def sums_copy(turn):
        rest = sums.at[turn, pl.ds(0, devices - 1)]
        return pltpu.make_async_remote_copy(
            src_ref=rest,
            dst_ref=rest,
            send_sem=sum_send.at[turn],
            recv_sem=sum_recv.at[turn],
            device_id={"col": peer_col(1)},
            device_id_type=MESH,
        )

    def finish_sums(turn, count):
        sums_copy(turn).wait_recv()
        total = jnp.broadcast_to(jnp.sum(sums[turn], axis=0), (8, 128))
        return [
            total if place == 0 else pltpu.roll(total, 128 - place * columns, 1)
            for place in range(count)
        ]

    lane = lax.broadcasted_iota(jnp.int32, (columns, 128), 1)
    row = lax.broadcasted_iota(jnp.int32, (columns, 128), 0)

    def by_column(lanes):
        wide = jnp.broadcast_to(lanes[:1], (columns, 128))
        picked = jnp.sum(jnp.where(lane == row, wide, 0.0), axis=1, keepdims=True)
        return jnp.broadcast_to(picked, (columns, 128))[None]

    loads[0].wait()
    start_exchange(0, potential0[...])
    for load in loads[1:]:
        load.wait()

    owner = member[...]
    drive = jnp.zeros(owner.shape, F32)
    for place in range(drive_s.shape[0]):
        drive = jnp.where(owner == place, drive_s[place], drive)
    panels[3] = drive
    for b in range(blocks):
        high, low = halves(precond_f[b].T)
        precond_w[b, :, :128] = high
        precond_w[b, :, 128:] = low

    for b in range(blocks):
        matrix_loads[b].wait()

        def prepare(k, carry, b=b):
            live = jnp.where(k < count_s[b], 1.0, 0.0).astype(F32)
            high, low = halves((staged[b, k] * live).T)
            place = pl.ds(pl.multiple_of(k * 128, 128), 128)
            weights[b, place, :128] = high
            weights[b, place, 128:] = low
            return carry

        lax.fori_loop(0, pairs, prepare, 0, unroll=4)

    def panel(place):
        return panels[place][:, None, :]

    def mismatch(field, near_value):
        grow = jnp.exp(ALPHA * field)
        shrink = jnp.exp(-BETA * field)
        value = (
            panel(0) * field
            + near_value
            + panel(1) * (grow - shrink)
            + panel(2) * (field - panel(3))
            - source_term[...]
        )
        slope = panel(1) * (ALPHA * grow + BETA * shrink) + panel(2)
        return value, slope

    def apply_precond(value):
        high, low = halves(value)
        left = jnp.concatenate([high, low], axis=1)
        return jnp.stack([both_halves(left[b], precond_w[b]) for b in range(blocks)])

    field = potential0[...]
    near_now = near_field(0)
    for newton in range(NEWTON):
        turn = 1 + 2 * newton
        value, slope = mismatch(field, near_now)
        p0 = -value
        z0 = apply_precond(p0)
        start_exchange(turn, z0)
        start_sums(2 * newton, [(p0, p0)])
        diagonal = panel(0) + slope
        n0 = near_field(turn)
        (g00,) = finish_sums(2 * newton, 1)
        beta2 = g00 + EPS
        beta = jnp.sqrt(beta2)
        unit = by_column(1.0 / beta)
        v0 = p0 * unit
        z0 = z0 * unit
        n0 = n0 * unit
        p1 = diagonal * z0 + n0
        z1 = apply_precond(p1)
        start_exchange(turn + 1, z1)
        n1 = near_field(turn + 1)
        p2 = diagonal * z1 + n1
        start_sums(
            2 * newton + 1, [(v0, p1), (p1, p1), (v0, p2), (p1, p2), (p2, p2)]
        )
        h00, g11, g02, g12, g22 = finish_sums(2 * newton + 1, 5)
        v00 = g00 / beta2
        pc = h00 - h00 * v00
        cc = jnp.maximum(g11 - h00 * h00 - h00 * pc, 0.0)
        pq = g02 - h00 * h00
        cq = g12 - h00 * g02 - h00 * (g11 - h00 * h00)
        qq = jnp.maximum(g22 - h00 * (2.0 * g12 - h00 * g11), 0.0)
        h10 = jnp.sqrt(cc + EPS)
        scale = 1.0 / h10
        scale2 = scale * scale
        v01 = pc * scale
        v11 = cc * scale2
        h01 = pq * scale
        w1 = cq * scale2
        h11 = w1 - h01 * v01
        square = (
            qq * scale2
            + h01 * h01 * v00
            + h11 * h11 * v11
            - 2.0 * h01 * h01
            - 2.0 * h11 * w1
            + 2.0 * h01 * h11 * v01
        )
        square = jnp.maximum(square, 0.0) + EPS
        gram0 = h00 * h00 + h10 * h10
        gram1 = h00 * h01 + h10 * h11
        gram2 = h01 * h01 + h11 * h11 + square
        lower0 = jnp.sqrt(gram0)
        lower1 = gram1 / lower0
        lower2 = jnp.sqrt(gram2 - lower1 * lower1)
        middle0 = beta * h00 / lower0
        middle1 = (beta * h01 - lower1 * middle0) / lower2
        y1 = middle1 / lower2
        y0 = (middle0 - lower1 * y1) / lower0
        a1 = y1 * scale
        a0 = by_column(y0 - a1 * h00)
        a1 = by_column(a1)
        field = field + (a0 * z0 + a1 * z1)
        near_now = near_now + (a0 * n0 + a1 * n1)
    potential_o[...] = field
    residual_o[...] = mismatch(field, near_now)[0]

    for turn in range(2 * NEWTON + 1):
        exchange_copy(turn).wait_send()
    for turn in range(2 * NEWTON):
        sums_copy(turn).wait_send()


def body(patches, cols, potential0, source_term, self_coef, nearfield, precond, exch_current, conductance, member, anode_drive, pair_source, pair_count):
    blocks, columns, panels = potential0.shape
    pairs = nearfield.shape[1]
    turns = 2 * NEWTON + 1
    slots = (cols + 2) * blocks
    hbm = pl.BlockSpec(memory_space=pltpu.HBM)
    vmem = pl.BlockSpec(memory_space=pltpu.VMEM)
    out = jax.ShapeDtypeStruct((blocks, columns, panels), F32)
    return pl.pallas_call(
        functools.partial(kernel, patches, cols),
        out_shape=(out, out),
        in_specs=[hbm] * 11,
        out_specs=(vmem, vmem),
        scratch_shapes=[
            pltpu.SMEM(anode_drive.shape, F32),
            pltpu.SMEM(pair_source.shape, jnp.int32),
            pltpu.SMEM(pair_count.shape, jnp.int32),
            pltpu.VMEM((blocks, columns, panels), F32),
            pltpu.VMEM((blocks, columns, panels), F32),
            pltpu.VMEM((4, blocks, panels), F32),
            pltpu.VMEM((blocks, panels), jnp.int32),
            pltpu.VMEM((blocks, pairs, panels, panels), F32),
            pltpu.VMEM((blocks, pairs * panels, 2 * panels), BF16),
            pltpu.VMEM((blocks, panels, panels), F32),
            pltpu.VMEM((blocks, panels, 2 * panels), BF16),
            pltpu.VMEM((turns, slots, columns, panels), F32),
            pltpu.VMEM((slots, 2 * columns, panels), BF16),
            pltpu.VMEM((2 * NEWTON, patches * cols, 1, 128), F32),
            pltpu.SemaphoreType.DMA((10 + blocks,)),
            pltpu.SemaphoreType.DMA((turns,)),
            pltpu.SemaphoreType.DMA((turns,)),
            pltpu.SemaphoreType.DMA((2 * NEWTON,)),
            pltpu.SemaphoreType.DMA((2 * NEWTON,)),
        ],
        compiler_params=pltpu.CompilerParams(
            collective_id=0, has_side_effects=True, vmem_limit_bytes=40 * 1024 * 1024
        ),
        name="newton_gmres",
    )(
        *(
            pltpu.with_memory_space_constraint(array, pltpu.HBM)
            for array in (
                anode_drive,
                pair_source,
                pair_count,
                potential0,
                source_term,
                self_coef,
                nearfield,
                precond,
                exch_current,
                conductance,
                member,
            )
        )
    )


def solution(mesh):
    both = ("patch", "col")
    return jax.shard_map(
        functools.partial(body, mesh.shape["patch"], mesh.shape["col"]),
        mesh=mesh,
        in_specs=(
            P(both, None, None),
            P(both, None, None),
            P(both, None),
            P(both, None, None, None),
            P(both, None, None),
            P(both, None),
            P(both, None),
            P(both, None),
            P(),
            P(both, None),
            P(both),
        ),
        out_specs=(P(both, None, None), P(both, None, None)),
        check_vma=False,
    )
```

time: 82.5 us -> 58.4 us (0.71)
  Pallas kernels: 70.2 us -> 56.4 us
  local copies, waits for them, and re-layouts: 11.2 us -> 1.23 us
    pallas_call x1, Pallas kernels: 70.2 us -> 56.4 us  [body(): pl.pallas_call(functools.partial(kernel, patches, cols), out_shape=(out,...]
    unnamed x24 -> x2, local copies, waits for them, and re-layouts: 11.2 us -> 1.23 us
where the time goes in v2:
time: 58.4 us; the launch traced here: 58.3 us
  Pallas kernels  56.4 us (97%)
  local copies, waits for them, and re-layouts  1.23 us (2%)
  between operations  0.64 us (1%)
    pallas_call x1, Pallas kernels, body(): pl.pallas_call(functools.partial(kernel, patches, cols), out_shape=(out,...  56.4 us
    unnamed x2, local copies, waits for them, and re-layouts  1.23 us

profile of v2, /device:TPU:1, one launch (start us, length us, event | category | flops | bytes accessed | tf_op | source)
XLA Modules:
  0.0 58.3 jit_solution(15536845668041200115)
XLA Ops:
  0.6 56.4 %newton_gmres.1 = (f32[4,16,128]{2,1,0:T(8,128)S(1)}, f32[4,16,128]{2,1,0:T(8,128)S(1)}) custom-call(f32[64]{0:T(128)} %drive_h.1, s32[4,24]{1,0:T(4,128)} %source_h.1, s32[4]{0:T(128)} %count_h.1, f32[4,16,128]{2,1,0:T(8,128)} %potential0_h.1, f32[4,16,128]{2,1,0:T(8,128)} %source_term_h.1, f32[4,128]{1,0:T(4,128)} %self_coef_h.1, ...), custom_call_target="tpu_custom_call" | custom-call | tf_op jit(solution)/shard_map/newton_gmres/pallas_call | solution.py:348
  57.0 0.6 %copy.15 = f32[4,16,128]{2,1,0:T(8,128)} copy(f32[4,16,128]{2,1,0:T(8,128)S(1)} %get-tuple-element.4) | data formatting | bytes 65536
  57.6 0.6 %copy.16 = f32[4,16,128]{2,1,0:T(8,128)} copy(f32[4,16,128]{2,1,0:T(8,128)S(1)} %get-tuple-element.5) | data formatting | bytes 65536

commit v3 on v2

--- a/solution.py
+++ b/solution.py
@@ -45,8 +45,7 @@
     current_h,
     conduct_h,
     member_h,
-    potential_o,
-    residual_o,
+    both_o,
     drive_s,
     source_s,
     count_s,
@@ -64,8 +63,11 @@
     load_sem,
     send_sem,
     recv_sem,
-    sum_send,
-    sum_recv,
+    sum_sem,
+    beta_a,
+    beta_b,
+    beta_sem,
+    entered_sem,
 ):
     patch = lax.axis_index("patch")
     col = lax.axis_index("col")
@@ -120,10 +122,24 @@
         return [(near_patch[p], near_col[c]) for p, c in steps]
 
     others = everyone()
+    side = 4
+    line, place = patch // side, lax.rem(patch, side)
+    col_peers = [{"col": peer_col(step)} for step in range(1, cols)]
+    y_peers = [
+        {"patch": lax.rem(line + step, patches // side) * side + place}
+        for step in range(1, patches // side)
+    ]
+    x_peers = [{"patch": line * side + lax.rem(place + step, side)} for step in range(1, side)]
+    next_peers = [{"patch": peer_patch(1)}, {"patch": peer_patch(patches - 1)}]
+
+    def signal_all(semaphore, targets):
+        for target in targets:
+            pl.semaphore_signal(semaphore, inc=1, device_id=target, device_id_type=MESH)
+
     barrier = pltpu.get_barrier_semaphore()
-    for target in others:
-        pl.semaphore_signal(barrier, inc=1, device_id=target, device_id_type=MESH)
-    pl.semaphore_wait(barrier, devices - 1)
+    greeted = x_peers + y_peers + next_peers + col_peers
+    signal_all(barrier, greeted)
+    pl.semaphore_wait(barrier, len(greeted))
 
     own = pl.ds(pl.multiple_of(col * blocks, blocks), blocks)
     before = pl.ds(cols * blocks, blocks)
@@ -172,34 +188,55 @@
             results.append(both_halves(left, weights[b]))
         return jnp.stack(results)
 
+    def spread(buffer, mine, semaphores, targets):
+        for target in targets:
+            pltpu.make_async_remote_copy(
+                src_ref=buffer.at[mine],
+                dst_ref=buffer.at[mine],
+                send_sem=semaphores.at[0],
+                recv_sem=semaphores.at[1],
+                device_id=target,
+                device_id_type=MESH,
+            ).start()
+
+    def spread_copy(buffer, semaphores):
+        rest = buffer.at[pl.ds(0, buffer.shape[0] - 1)]
+        return pltpu.make_async_remote_copy(
+            src_ref=rest,
+            dst_ref=rest,
+            send_sem=semaphores.at[0],
+            recv_sem=semaphores.at[1],
+            device_id={"col": peer_col(1)},
+            device_id_type=MESH,
+        )
+
+    patch_peers = [{"patch": peer_patch(step)} for step in range(1, patches)]
+
+    def start_beta(newton, value):
+        table = jnp.concatenate(
+            [jnp.sum(value * value, axis=0), jnp.zeros((128 - columns, 128), F32)], axis=0
+        )
+        beta_a[newton, patch] = jnp.sum(table.T, axis=0, keepdims=True)
+        spread(beta_a.at[newton], patch, beta_sem.at[newton, 0], patch_peers)
+
+    def pass_beta(newton):
+        spread_copy(beta_a.at[newton], beta_sem.at[newton, 0]).wait_recv()
+        beta_b[newton, col] = jnp.sum(beta_a[newton], axis=0)
+        spread(beta_b.at[newton], col, beta_sem.at[newton, 1], col_peers)
+
+    def finish_beta(newton):
+        spread_copy(beta_b.at[newton], beta_sem.at[newton, 1]).wait_recv()
+        return jnp.broadcast_to(jnp.sum(beta_b[newton], axis=0), (8, 128))
+
     def start_sums(turn, parts):
         rows = [jnp.sum(left * right, axis=0) for left, right in parts]
         rows.append(jnp.zeros((128 - len(parts) * columns, 128), F32))
         table = jnp.concatenate(rows, axis=0)
         sums[turn, me] = jnp.sum(table.T, axis=0, keepdims=True)
-        for target in others:
-            pltpu.make_async_remote_copy(
-                src_ref=sums.at[turn, me],
-                dst_ref=sums.at[turn, me],
-                send_sem=sum_send.at[turn],
-                recv_sem=sum_recv.at[turn],
-                device_id=target,
-                device_id_type=MESH,
-            ).start()
-
-    def sums_copy(turn):
-        rest = sums.at[turn, pl.ds(0, devices - 1)]
-        return pltpu.make_async_remote_copy(
-            src_ref=rest,
-            dst_ref=rest,
-            send_sem=sum_send.at[turn],
-            recv_sem=sum_recv.at[turn],
-            device_id={"col": peer_col(1)},
-            device_id_type=MESH,
-        )
+        spread(sums.at[turn], me, sum_sem.at[turn], others)
 
     def finish_sums(turn, count):
-        sums_copy(turn).wait_recv()
+        spread_copy(sums.at[turn], sum_sem.at[turn]).wait_recv()
         total = jnp.broadcast_to(jnp.sum(sums[turn], axis=0), (8, 128))
         return [
             total if place == 0 else pltpu.roll(total, 128 - place * columns, 1)
@@ -216,6 +253,7 @@
 
     loads[0].wait()
     start_exchange(0, potential0[...])
+    signal_all(entered_sem.at[0], x_peers)
     for load in loads[1:]:
         load.wait()
 
@@ -263,33 +301,35 @@
         left = jnp.concatenate([high, low], axis=1)
         return jnp.stack([both_halves(left[b], precond_w[b]) for b in range(blocks)])
 
+    pl.semaphore_wait(entered_sem.at[0], len(x_peers))
+    signal_all(entered_sem.at[1], col_peers)
     field = potential0[...]
     near_now = near_field(0)
+    pl.semaphore_wait(entered_sem.at[1], len(col_peers))
     for newton in range(NEWTON):
         turn = 1 + 2 * newton
         value, slope = mismatch(field, near_now)
         p0 = -value
         z0 = apply_precond(p0)
         start_exchange(turn, z0)
-        start_sums(2 * newton, [(p0, p0)])
+        start_beta(newton, p0)
         diagonal = panel(0) + slope
         n0 = near_field(turn)
-        (g00,) = finish_sums(2 * newton, 1)
+        p1 = diagonal * z0 + n0
+        z1 = apply_precond(p1)
+        start_exchange(turn + 1, z1)
+        pass_beta(newton)
+        n1 = near_field(turn + 1)
+        p2 = diagonal * z1 + n1
+        g00 = finish_beta(newton)
         beta2 = g00 + EPS
         beta = jnp.sqrt(beta2)
         unit = by_column(1.0 / beta)
-        v0 = p0 * unit
-        z0 = z0 * unit
-        n0 = n0 * unit
-        p1 = diagonal * z0 + n0
-        z1 = apply_precond(p1)
-        start_exchange(turn + 1, z1)
-        n1 = near_field(turn + 1)
-        p2 = diagonal * z1 + n1
+        v0, p1, p2 = p0 * unit, p1 * unit, p2 * unit
         start_sums(
-            2 * newton + 1, [(v0, p1), (p1, p1), (v0, p2), (p1, p2), (p2, p2)]
-        )
-        h00, g11, g02, g12, g22 = finish_sums(2 * newton + 1, 5)
+            newton, [(v0, p1), (p1, p1), (v0, p2), (p1, p2), (p2, p2)]
+        )
+        h00, g11, g02, g12, g22 = finish_sums(newton, 5)
         v00 = g00 / beta2
         pc = h00 - h00 * v00
         cc = jnp.maximum(g11 - h00 * h00 - h00 * pc, 0.0)
@@ -324,17 +364,19 @@
         y1 = middle1 / lower2
         y0 = (middle0 - lower1 * y1) / lower0
         a1 = y1 * scale
-        a0 = by_column(y0 - a1 * h00)
-        a1 = by_column(a1)
+        a0 = by_column((y0 - a1 * h00) / beta)
+        a1 = by_column(a1 / beta)
         field = field + (a0 * z0 + a1 * z1)
         near_now = near_now + (a0 * n0 + a1 * n1)
-    potential_o[...] = field
-    residual_o[...] = mismatch(field, near_now)[0]
+    both_o[0] = field
+    both_o[1] = mismatch(field, near_now)[0]
 
     for turn in range(2 * NEWTON + 1):
         exchange_copy(turn).wait_send()
-    for turn in range(2 * NEWTON):
-        sums_copy(turn).wait_send()
+    for newton in range(NEWTON):
+        spread_copy(sums.at[newton], sum_sem.at[newton]).wait_send()
+        spread_copy(beta_a.at[newton], beta_sem.at[newton, 0]).wait_send()
+        spread_copy(beta_b.at[newton], beta_sem.at[newton, 1]).wait_send()
 
 
 def body(patches, cols, potential0, source_term, self_coef, nearfield, precond, exch_current, conductance, member, anode_drive, pair_source, pair_count):
@@ -344,12 +386,12 @@
     slots = (cols + 2) * blocks
     hbm = pl.BlockSpec(memory_space=pltpu.HBM)
     vmem = pl.BlockSpec(memory_space=pltpu.VMEM)
-    out = jax.ShapeDtypeStruct((blocks, columns, panels), F32)
-    return pl.pallas_call(
+    out = jax.ShapeDtypeStruct((2, blocks, columns, panels), F32)
+    both = pl.pallas_call(
         functools.partial(kernel, patches, cols),
-        out_shape=(out, out),
+        out_shape=out,
         in_specs=[hbm] * 11,
-        out_specs=(vmem, vmem),
+        out_specs=vmem,
         scratch_shapes=[
             pltpu.SMEM(anode_drive.shape, F32),
             pltpu.SMEM(pair_source.shape, jnp.int32),
@@ -364,12 +406,15 @@
             pltpu.VMEM((blocks, panels, 2 * panels), BF16),
             pltpu.VMEM((turns, slots, columns, panels), F32),
             pltpu.VMEM((slots, 2 * columns, panels), BF16),
-            pltpu.VMEM((2 * NEWTON, patches * cols, 1, 128), F32),
+            pltpu.VMEM((NEWTON, patches * cols, 1, 128), F32),
             pltpu.SemaphoreType.DMA((10 + blocks,)),
             pltpu.SemaphoreType.DMA((turns,)),
             pltpu.SemaphoreType.DMA((turns,)),
-            pltpu.SemaphoreType.DMA((2 * NEWTON,)),
-            pltpu.SemaphoreType.DMA((2 * NEWTON,)),
+            pltpu.SemaphoreType.DMA((NEWTON, 2)),
+            pltpu.VMEM((NEWTON, patches, 1, 128), F32),
+            pltpu.VMEM((NEWTON, cols, 1, 128), F32),
+            pltpu.SemaphoreType.DMA((NEWTON, 2, 2)),
+            pltpu.SemaphoreType.REGULAR((2,)),
         ],
         compiler_params=pltpu.CompilerParams(
             collective_id=0, has_side_effects=True, vmem_limit_bytes=40 * 1024 * 1024
@@ -393,6 +438,7 @@
             )
         )
     )
+    return both[0], both[1]
 
 
 def solution(mesh):

time: 58.4 us -> 53.7 us (0.920)
  Pallas kernels: 56.4 us -> 52.4 us
  local copies, waits for them, and re-layouts: 1.23 us -> 0.63 us
    pallas_call x1, Pallas kernels: 56.4 us -> 52.4 us  [body(): pl.pallas_call(functools.partial(kernel, patches, cols), out_shape=out, i...]
    unnamed x2 -> x0, local copies, waits for them, and re-layouts: 1.23 us -> none
    squeeze x0 -> x1, local copies, waits for them, and re-layouts: none -> 0.63 us  [body(): return (both[0], both[1])]
where the time goes in v3:
time: 53.7 us; the launch traced here: 53.6 us
  Pallas kernels  52.4 us (98%)
  between operations  0.64 us (1%)
  local copies, waits for them, and re-layouts  0.63 us (1%)
    pallas_call x1, Pallas kernels, body(): pl.pallas_call(functools.partial(kernel, patches, cols), out_shape=out, i...  52.4 us

profile of v3, /device:TPU:1, one launch (start us, length us, event | category | flops | bytes accessed | tf_op | source)
XLA Modules:
  0.0 53.6 jit_solution(17272076956400479155)
XLA Ops:
  0.6 52.4 %newton_gmres.1 = f32[2,4,16,128]{3,2,1,0:T(8,128)S(1)} custom-call(f32[64]{0:T(128)} %drive_h.1, s32[4,24]{1,0:T(4,128)} %source_h.1, s32[4]{0:T(128)} %count_h.1, f32[4,16,128]{2,1,0:T(8,128)} %potential0_h.1, f32[4,16,128]{2,1,0:T(8,128)} %source_term_h.1, f32[4,128]{1,0:T(4,128)} %self_coef_h.1, f32[4,24,128,128]{3,2,1,0:T(8,128)} %nearfield_h.1, ...), custom_call_target="tpu_custom_call" | custom-call | tf_op jit(solution)/shard_map/newton_gmres/pallas_call | solution.py:390
  53.0 0.6 %slice_bitcast_fusion = (f32[4,16,128]{2,1,0:T(8,128)}, f32[4,16,128]{2,1,0:T(8,128)}) fusion(f32[2,4,16,128]{3,2,1,0:T(8,128)S(1)} %newton_gmres.1), kind=kLoop, calls=%fused_computation | loop fusion | bytes 131072 | tf_op jit(solution)/shard_map/squeeze | solution.py:441

commit v4 on v3

--- a/solution.py
+++ b/solution.py
@@ -75,6 +75,52 @@
     columns = potential0.shape[1]
     slots = exchange.shape[1]
 
+    me = patch * cols + col
+    devices = patches * cols
+
+    def peer_col(step):
+        return lax.rem(col + step, cols)
+
+    def peer_patch(step):
+        return lax.rem(patch + step, patches)
+
+    def everyone():
+        def distance(step, size):
+            return min(step, size - step)
+
+        steps = [(p, c) for p in range(patches) for c in range(cols) if p or c]
+        side = 4
+        steps.sort(
+            key=lambda s: (
+                distance(s[0] // side, patches // side)
+                + distance(s[0] % side, side)
+                + distance(s[1] // 2, cols // 2)
+            ),
+            reverse=True,
+        )
+        near_patch = [peer_patch(p) for p in range(patches)]
+        near_col = [peer_col(c) for c in range(cols)]
+        return [(near_patch[p], near_col[c]) for p, c in steps]
+
+    others = everyone()
+    side = 4
+    line, place = patch // side, lax.rem(patch, side)
+    col_peers = [{"col": peer_col(step)} for step in range(1, cols)]
+    y_peers = [
+        {"patch": lax.rem(line + step, patches // side) * side + place}
+        for step in range(1, patches // side)
+    ]
+    x_peers = [{"patch": line * side + lax.rem(place + step, side)} for step in range(1, side)]
+    next_peers = [{"patch": peer_patch(1)}, {"patch": peer_patch(patches - 1)}]
+
+    def signal_all(semaphore, targets):
+        for target in targets:
+            pl.semaphore_signal(semaphore, inc=1, device_id=target, device_id_type=MESH)
+
+    barrier = pltpu.get_barrier_semaphore()
+    greeted = x_peers + y_peers + next_peers + col_peers
+    signal_all(barrier, greeted)
+
     loads = [
         pltpu.make_async_copy(potential0_h, potential0, load_sem.at[0]),
         pltpu.make_async_copy(source_term_h, source_term, load_sem.at[1]),
@@ -94,51 +140,6 @@
     for load in loads + matrix_loads:
         load.start()
 
-    me = patch * cols + col
-    devices = patches * cols
-
-    def peer_col(step):
-        return lax.rem(col + step, cols)
-
-    def peer_patch(step):
-        return lax.rem(patch + step, patches)
-
-    def everyone():
-        def distance(step, size):
-            return min(step, size - step)
-
-        steps = [(p, c) for p in range(patches) for c in range(cols) if p or c]
-        side = 4
-        steps.sort(
-            key=lambda s: (
-                distance(s[0] // side, patches // side)
-                + distance(s[0] % side, side)
-                + distance(s[1] // 2, cols // 2)
-            ),
-            reverse=True,
-        )
-        near_patch = [peer_patch(p) for p in range(patches)]
-        near_col = [peer_col(c) for c in range(cols)]
-        return [(near_patch[p], near_col[c]) for p, c in steps]
-
-    others = everyone()
-    side = 4
-    line, place = patch // side, lax.rem(patch, side)
-    col_peers = [{"col": peer_col(step)} for step in range(1, cols)]
-    y_peers = [
-        {"patch": lax.rem(line + step, patches // side) * side + place}
-        for step in range(1, patches // side)
-    ]
-    x_peers = [{"patch": line * side + lax.rem(place + step, side)} for step in range(1, side)]
-    next_peers = [{"patch": peer_patch(1)}, {"patch": peer_patch(patches - 1)}]
-
-    def signal_all(semaphore, targets):
-        for target in targets:
-            pl.semaphore_signal(semaphore, inc=1, device_id=target, device_id_type=MESH)
-
-    barrier = pltpu.get_barrier_semaphore()
-    greeted = x_peers + y_peers + next_peers + col_peers
-    signal_all(barrier, greeted)
     pl.semaphore_wait(barrier, len(greeted))
 
     own = pl.ds(pl.multiple_of(col * blocks, blocks), blocks)
@@ -176,8 +177,9 @@
             device_id_type=MESH,
         )
 
-    def near_field(turn):
+    def near_field(turn, then=lambda: None):
         exchange_copy(turn).wait_recv()
+        then()
         high, low = halves(exchange[turn])
         split[:, :columns] = high
         split[:, columns:] = low
@@ -228,10 +230,12 @@
         spread_copy(beta_b.at[newton], beta_sem.at[newton, 1]).wait_recv()
         return jnp.broadcast_to(jnp.sum(beta_b[newton], axis=0), (8, 128))
 
+    def products(left, right):
+        return jnp.sum(left * right, axis=0)
+
     def start_sums(turn, parts):
-        rows = [jnp.sum(left * right, axis=0) for left, right in parts]
-        rows.append(jnp.zeros((128 - len(parts) * columns, 128), F32))
-        table = jnp.concatenate(rows, axis=0)
+        rest = jnp.zeros((128 - len(parts) * columns, 128), F32)
+        table = jnp.concatenate(parts + [rest], axis=0)
         sums[turn, me] = jnp.sum(table.T, axis=0, keepdims=True)
         spread(sums.at[turn], me, sum_sem.at[turn], others)
 
@@ -314,58 +318,45 @@
         start_exchange(turn, z0)
         start_beta(newton, p0)
         diagonal = panel(0) + slope
-        n0 = near_field(turn)
+        n0 = near_field(turn, lambda: pass_beta(newton))
         p1 = diagonal * z0 + n0
         z1 = apply_precond(p1)
         start_exchange(turn + 1, z1)
-        pass_beta(newton)
-        n1 = near_field(turn + 1)
-        p2 = diagonal * z1 + n1
         g00 = finish_beta(newton)
         beta2 = g00 + EPS
         beta = jnp.sqrt(beta2)
         unit = by_column(1.0 / beta)
-        v0, p1, p2 = p0 * unit, p1 * unit, p2 * unit
-        start_sums(
-            newton, [(v0, p1), (p1, p1), (v0, p2), (p1, p2), (p2, p2)]
-        )
+        v0, p1, direct = p0 * unit, p1 * unit, diagonal * z1 * unit
+        parts = [products(v0, p1), products(p1, p1)]
+        n1 = near_field(turn + 1)
+        p2 = direct + n1 * unit
+        parts += [products(v0, p2), products(p1, p2), products(p2, p2)]
+        start_sums(newton, parts)
         h00, g11, g02, g12, g22 = finish_sums(newton, 5)
         v00 = g00 / beta2
         pc = h00 - h00 * v00
+        pq = g02 - h00 * h00
         cc = jnp.maximum(g11 - h00 * h00 - h00 * pc, 0.0)
-        pq = g02 - h00 * h00
         cq = g12 - h00 * g02 - h00 * (g11 - h00 * h00)
         qq = jnp.maximum(g22 - h00 * (2.0 * g12 - h00 * g11), 0.0)
-        h10 = jnp.sqrt(cc + EPS)
-        scale = 1.0 / h10
-        scale2 = scale * scale
-        v01 = pc * scale
-        v11 = cc * scale2
-        h01 = pq * scale
-        w1 = cq * scale2
-        h11 = w1 - h01 * v01
+        norm2 = cc + EPS
+        gram0 = h00 * h00 + norm2
+        over_norm = 1.0 / norm2
+        over_gram = 1.0 / gram0
+        cross = cq - pq * pc
+        ratio = cross * over_norm
         square = (
-            qq * scale2
-            + h01 * h01 * v00
-            + h11 * h11 * v11
-            - 2.0 * h01 * h01
-            - 2.0 * h11 * w1
-            + 2.0 * h01 * h11 * v01
-        )
-        square = jnp.maximum(square, 0.0) + EPS
-        gram0 = h00 * h00 + h10 * h10
-        gram1 = h00 * h01 + h10 * h11
-        gram2 = h01 * h01 + h11 * h11 + square
-        lower0 = jnp.sqrt(gram0)
-        lower1 = gram1 / lower0
-        lower2 = jnp.sqrt(gram2 - lower1 * lower1)
-        middle0 = beta * h00 / lower0
-        middle1 = (beta * h01 - lower1 * middle0) / lower2
-        y1 = middle1 / lower2
-        y0 = (middle0 - lower1 * y1) / lower0
-        a1 = y1 * scale
-        a0 = by_column((y0 - a1 * h00) / beta)
-        a1 = by_column(a1 / beta)
+            qq
+            + pq * pq * (v00 - 2.0)
+            + ratio * (ratio * cc - 2.0 * cq + 2.0 * pq * pc)
+        )
+        square = jnp.maximum(square, 0.0) + EPS * norm2
+        across = norm2 * pq - h00 * cross
+        part = across * over_gram
+        y1 = part / (square + part * (across * over_norm))
+        y0 = (h00 - (h00 * pq + cross) * y1) * over_gram
+        a0 = by_column(y0 - y1 * h00)
+        a1 = by_column(y1)
         field = field + (a0 * z0 + a1 * z1)
         near_now = near_now + (a0 * n0 + a1 * n1)
     both_o[0] = field

time: 53.7 us -> 53.6 us (level)
  no operation moved by 1% of the time
where the time goes in v4:
time: 53.6 us; the launch traced here: 53.5 us
  Pallas kernels  52.2 us (97%)
  between operations  0.64 us (1%)
  local copies, waits for them, and re-layouts  0.63 us (1%)
    pallas_call x1, Pallas kernels, body(): pl.pallas_call(functools.partial(kernel, patches, cols), out_shape=out, i...  52.2 us

profile of v4, /device:TPU:1, one launch (start us, length us, event | category | flops | bytes accessed | tf_op | source)
XLA Modules:
  0.0 53.5 jit_solution(7602552553825007077)
XLA Ops:
  0.6 52.2 %newton_gmres.1 = f32[2,4,16,128]{3,2,1,0:T(8,128)S(1)} custom-call(f32[64]{0:T(128)} %drive_h.1, s32[4,24]{1,0:T(4,128)} %source_h.1, s32[4]{0:T(128)} %count_h.1, f32[4,16,128]{2,1,0:T(8,128)} %potential0_h.1, f32[4,16,128]{2,1,0:T(8,128)} %source_term_h.1, f32[4,128]{1,0:T(4,128)} %self_coef_h.1, f32[4,24,128,128]{3,2,1,0:T(8,128)} %nearfield_h.1, ...), custom_call_target="tpu_custom_call" | custom-call | tf_op jit(solution)/shard_map/newton_gmres/pallas_call | solution.py:381
  52.9 0.6 %slice_bitcast_fusion = (f32[4,16,128]{2,1,0:T(8,128)}, f32[4,16,128]{2,1,0:T(8,128)}) fusion(f32[2,4,16,128]{3,2,1,0:T(8,128)S(1)} %newton_gmres.1), kind=kLoop, calls=%fused_computation | loop fusion | bytes 131072 | tf_op jit(solution)/shard_map/squeeze | solution.py:432

commit v5 on v4

--- a/solution.py
+++ b/solution.py
@@ -145,44 +145,75 @@
     own = pl.ds(pl.multiple_of(col * blocks, blocks), blocks)
     before = pl.ds(cols * blocks, blocks)
     after = pl.ds((cols + 1) * blocks, blocks)
-    incoming = pl.ds(0, slots - blocks)
+    half = blocks // 2
+    core = lax.rem(col, 2)
+    chips = cols // 2
+    far_chip = lax.rem(col // 2 + chips // 2, chips)
+    sibling = {"col": col + 1 - 2 * core}
+    near_cols = [lax.rem(col // 2 + step, chips) * 2 for step in (1, chips - 1)]
+    near_targets = [{"col": near + side_core} for near in near_cols for side_core in range(2)]
+    near_targets.append(sibling)
 
     def start_exchange(turn, value):
         exchange[turn, own] = value
-        mine = exchange.at[turn, own]
-
-        def send(place, target):
+
+        def send(kind, source, place, target):
             pltpu.make_async_remote_copy(
-                src_ref=mine,
+                src_ref=exchange.at[turn, source],
                 dst_ref=exchange.at[turn, place],
                 send_sem=send_sem.at[turn],
-                recv_sem=recv_sem.at[turn],
+                recv_sem=recv_sem.at[turn, kind],
                 device_id=target,
                 device_id_type=MESH,
             ).start()
 
-        steps = sorted(range(1, cols), key=lambda s: -min(s // 2, cols // 2 - s // 2))
-        for step in steps:
-            send(own, {"col": peer_col(step)})
-        send(before, {"patch": peer_patch(1)})
-        send(after, {"patch": peer_patch(patches - 1)})
-
-    def exchange_copy(turn):
+        for side_core in range(2):
+            piece = pl.ds(col * blocks + side_core * half, half)
+            send(1, piece, piece, {"col": far_chip * 2 + side_core})
+        for target in near_targets:
+            send(0, own, own, target)
+        send(0, own, before, next_peers[0])
+        send(0, own, after, next_peers[1])
+
+    def exchange_copy(turn, kind, count):
         return pltpu.make_async_remote_copy(
-            src_ref=exchange.at[turn, incoming],
-            dst_ref=exchange.at[turn, incoming],
+            src_ref=exchange.at[turn, pl.ds(0, count)],
+            dst_ref=exchange.at[turn, pl.ds(0, count)],
             send_sem=send_sem.at[turn],
-            recv_sem=recv_sem.at[turn],
-            device_id={"col": peer_col(1)},
+            recv_sem=recv_sem.at[turn, kind],
+            device_id=sibling,
             device_id_type=MESH,
         )
 
+    def split_slots(turn, first, count):
+        place = pl.ds(first, count)
+        high, low = halves(exchange[turn, place])
+        split[place, :columns] = high
+        split[place, columns:] = low
+
+    def receive(turn):
+        exchange_copy(turn, 1, 2 * half).wait_recv()
+        for side_core in range(2):
+            piece = pl.ds((far_chip * 2 + side_core) * blocks + core * half, half)
+            pltpu.make_async_remote_copy(
+                src_ref=exchange.at[turn, piece],
+                dst_ref=exchange.at[turn, piece],
+                send_sem=send_sem.at[turn],
+                recv_sem=recv_sem.at[turn, 2],
+                device_id=sibling,
+                device_id_type=MESH,
+            ).start()
+        exchange_copy(turn, 0, slots - 3 * blocks).wait_recv()
+        group = 2 * blocks
+        for step in range(1, chips):
+            split_slots(turn, lax.rem(far_chip + step, chips) * group, group)
+        split_slots(turn, cols * blocks, group)
+        exchange_copy(turn, 2, 2 * half).wait_recv()
+        split_slots(turn, far_chip * group, group)
+
     def near_field(turn, then=lambda: None):
-        exchange_copy(turn).wait_recv()
+        receive(turn)
         then()
-        high, low = halves(exchange[turn])
-        split[:, :columns] = high
-        split[:, columns:] = low
 
         results = []
         for b in range(blocks):
@@ -363,7 +394,7 @@
     both_o[1] = mismatch(field, near_now)[0]
 
     for turn in range(2 * NEWTON + 1):
-        exchange_copy(turn).wait_send()
+        exchange_copy(turn, 0, slots - blocks).wait_send()
     for newton in range(NEWTON):
         spread_copy(sums.at[newton], sum_sem.at[newton]).wait_send()
         spread_copy(beta_a.at[newton], beta_sem.at[newton, 0]).wait_send()
@@ -400,7 +431,7 @@
             pltpu.VMEM((NEWTON, patches * cols, 1, 128), F32),
             pltpu.SemaphoreType.DMA((10 + blocks,)),
             pltpu.SemaphoreType.DMA((turns,)),
-            pltpu.SemaphoreType.DMA((turns,)),
+            pltpu.SemaphoreType.DMA((turns, 3)),
             pltpu.SemaphoreType.DMA((NEWTON, 2)),
             pltpu.VMEM((NEWTON, patches, 1, 128), F32),
             pltpu.VMEM((NEWTON, cols, 1, 128), F32),

time: 53.6 us -> 53 us (0.989)
  Pallas kernels: 52.2 us -> 51.6 us
    pallas_call x1, Pallas kernels: 52.2 us -> 51.6 us  [body(): pl.pallas_call(functools.partial(kernel, patches, cols), out_shape=out, i...]
where the time goes in v5:
time: 53 us; the launch traced here: 52.9 us
  Pallas kernels  51.6 us (97%)
  between operations  0.64 us (1%)
  local copies, waits for them, and re-layouts  0.63 us (1%)
    pallas_call x1, Pallas kernels, body(): pl.pallas_call(functools.partial(kernel, patches, cols), out_shape=out, i...  51.6 us

profile of v5, /device:TPU:1, one launch (start us, length us, event | category | flops | bytes accessed | tf_op | source)
XLA Modules:
  0.0 52.9 jit_solution(17306641222440479904)
XLA Ops:
  0.6 51.6 %newton_gmres.1 = f32[2,4,16,128]{3,2,1,0:T(8,128)S(1)} custom-call(f32[64]{0:T(128)} %drive_h.1, s32[4,24]{1,0:T(4,128)} %source_h.1, s32[4]{0:T(128)} %count_h.1, f32[4,16,128]{2,1,0:T(8,128)} %potential0_h.1, f32[4,16,128]{2,1,0:T(8,128)} %source_term_h.1, f32[4,128]{1,0:T(4,128)} %self_coef_h.1, f32[4,24,128,128]{3,2,1,0:T(8,128)} %nearfield_h.1, ...), custom_call_target="tpu_custom_call" | custom-call | tf_op jit(solution)/shard_map/newton_gmres/pallas_call | solution.py:412
  52.3 0.6 %slice_bitcast_fusion = (f32[4,16,128]{2,1,0:T(8,128)}, f32[4,16,128]{2,1,0:T(8,128)}) fusion(f32[2,4,16,128]{3,2,1,0:T(8,128)S(1)} %newton_gmres.1), kind=kLoop, calls=%fused_computation | loop fusion | bytes 131072 | tf_op jit(solution)/shard_map/squeeze | solution.py:463

commit v6 on v5

--- a/solution.py
+++ b/solution.py
@@ -170,10 +170,10 @@
         for side_core in range(2):
             piece = pl.ds(col * blocks + side_core * half, half)
             send(1, piece, piece, {"col": far_chip * 2 + side_core})
+        send(0, own, before, next_peers[0])
+        send(0, own, after, next_peers[1])
         for target in near_targets:
             send(0, own, own, target)
-        send(0, own, before, next_peers[0])
-        send(0, own, after, next_peers[1])
 
     def exchange_copy(turn, kind, count):
         return pltpu.make_async_remote_copy(
@@ -191,7 +191,7 @@
         split[place, :columns] = high
         split[place, columns:] = low
 
-    def receive(turn):
+    def receive(turn, then):
         exchange_copy(turn, 1, 2 * half).wait_recv()
         for side_core in range(2):
             piece = pl.ds((far_chip * 2 + side_core) * blocks + core * half, half)
@@ -208,12 +208,12 @@
         for step in range(1, chips):
             split_slots(turn, lax.rem(far_chip + step, chips) * group, group)
         split_slots(turn, cols * blocks, group)
+        then()
         exchange_copy(turn, 2, 2 * half).wait_recv()
         split_slots(turn, far_chip * group, group)
 
     def near_field(turn, then=lambda: None):
-        receive(turn)
-        then()
+        receive(turn, then)
 
         results = []
         for b in range(blocks):

time: 53 us -> 52.9 us (level)
  no operation moved by 1% of the time
where the time goes in v6:
time: 52.9 us; the launch traced here: 52.8 us
  Pallas kernels  51.5 us (97%)
  between operations  0.64 us (1%)
  local copies, waits for them, and re-layouts  0.63 us (1%)
    pallas_call x1, Pallas kernels, body(): pl.pallas_call(functools.partial(kernel, patches, cols), out_shape=out, i...  51.5 us

profile of v6, /device:TPU:1, one launch (start us, length us, event | category | flops | bytes accessed | tf_op | source)
XLA Modules:
  0.0 52.8 jit_solution(4594443760125922453)
XLA Ops:
  0.6 51.5 %newton_gmres.1 = f32[2,4,16,128]{3,2,1,0:T(8,128)S(1)} custom-call(f32[64]{0:T(128)} %drive_h.1, s32[4,24]{1,0:T(4,128)} %source_h.1, s32[4]{0:T(128)} %count_h.1, f32[4,16,128]{2,1,0:T(8,128)} %potential0_h.1, f32[4,16,128]{2,1,0:T(8,128)} %source_term_h.1, f32[4,128]{1,0:T(4,128)} %self_coef_h.1, f32[4,24,128,128]{3,2,1,0:T(8,128)} %nearfield_h.1, ...), custom_call_target="tpu_custom_call" | custom-call | tf_op jit(solution)/shard_map/newton_gmres/pallas_call | solution.py:412
  52.2 0.6 %slice_bitcast_fusion = (f32[4,16,128]{2,1,0:T(8,128)}, f32[4,16,128]{2,1,0:T(8,128)}) fusion(f32[2,4,16,128]{3,2,1,0:T(8,128)S(1)} %newton_gmres.1), kind=kLoop, calls=%fused_computation | loop fusion | bytes 131072 | tf_op jit(solution)/shard_map/squeeze | solution.py:463
